TPU v7x, 32 devices: a whole 2x2x4 slice. The times are simulated.
32 devices in a mesh: replica: 8 (over y, x, core), fsdp: 4 (over z).
Axes of the slice: x: 2, y: 2, z: 4, core: 2. Of those that a mesh axis runs over, the one named last changes fastest.
Arguments:
- hidden_in: bfloat16 [9216, 768], P(('replica', 'fsdp')), may hold values from -6 to 6
- segments: int32 [32, 288], P(('replica', 'fsdp')), may hold values from 0 to 18, as said below
- positions: int32 [32, 288], P(('replica', 'fsdp')), may hold values from 0 to 287, as said below
- attn_gain: bfloat16 [768], P('fsdp'), may hold values from 0.25 to 1.75
- attn_shift: bfloat16 [768], P('fsdp'), may hold values from -3 to 3
- mlp_gain: bfloat16 [768], P('fsdp'), may hold values from 0.25 to 1.75
- mlp_shift: bfloat16 [768], P('fsdp'), may hold values from -3 to 3
- w_qkv: bfloat16 [768, 2304], P('fsdp'), may hold values from -0.21875 to 0.21875
- q_bias: bfloat16 [768], P('fsdp'), may hold values from -3 to 3
- v_bias: bfloat16 [768], P('fsdp'), may hold values from -3 to 3
- w_out: bfloat16 [768, 768], P('fsdp'), may hold values from -0.875 to 0.875
- w_up: bfloat16 [768, 3072], P('fsdp'), may hold values from -0.21875 to 0.21875
- up_bias: bfloat16 [3072], P('fsdp'), may hold values from -3 to 3
- w_down: bfloat16 [3072, 768], P('fsdp'), may hold values from -0.109375 to 0.109375
- out_bias: bfloat16 [768], P('fsdp'), may hold values from -3 to 3
- cotangent: bfloat16 [9216, 768], P(('replica', 'fsdp')), may hold values from -6 to 6
Outputs:
- layer_out: bfloat16 [9216, 768], P(('replica', 'fsdp'))
- grad_in: bfloat16 [9216, 768], P(('replica', 'fsdp'))
- grad_attn_gain: float32 [768], P('fsdp')
- grad_attn_shift: float32 [768], P('fsdp')
- grad_mlp_gain: float32 [768], P('fsdp')
- grad_mlp_shift: float32 [768], P('fsdp')
- grad_w_qkv: float32 [768, 2304], P('fsdp')
- grad_q_bias: float32 [768], P('fsdp')
- grad_v_bias: float32 [768], P('fsdp')
- grad_w_out: float32 [768, 768], P('fsdp')
- grad_w_up: float32 [768, 3072], P('fsdp')
- grad_up_bias: float32 [3072], P('fsdp')
- grad_w_down: float32 [3072, 768], P('fsdp')
- grad_out_bias: float32 [768], P('fsdp')
Inputs may be any that keep to these rules, and one draw needn't show every extreme that they name: `segments`: along each row the document numbers start at 0 and rise by one at each new document; a token attends to itself and the earlier tokens of its row with the same number; a document that neither begins nor ends its row has 16 or more tokens. `positions`: A token's index within its document.
All inputs are finite; a program needn't handle non-finite values.
Results may differ from a plain program's by a relative error of at most 0.019.
Values may be sent and summed in bfloat16 or wider, within the bound.
No kernel may reach another device: no remote copies, remote signals or barrier semaphores. Data moves between devices by JAX's collectives and lax.ppermute only.
A program may use at most 128 MiB of HBM per device.

v0:
```python
import math
import jax
import jax.numpy as jnp
from jax import lax
from jax.sharding import PartitionSpec as P

HD = 64
ROT = 16
EPSILON = 1e-05


def normalize(x_f32):
    center = x_f32 - jnp.mean(x_f32, axis=-1, keepdims=True)
    inv_dev = lax.rsqrt(jnp.mean(center * center, axis=-1, keepdims=True) + EPSILON)
    return (center * inv_dev, inv_dev)


def angles(positions, rot_dims):
    half_rot = rot_dims // 2
    frequency = jnp.power(10000.0, -jnp.arange(half_rot, dtype=jnp.float32) * (2.0 / rot_dims))
    phase_angle = positions.astype(jnp.float32)[..., None] * frequency
    phase_angle = jnp.concatenate([phase_angle, phase_angle], axis=-1)[:, :, None, :]
    return (jnp.cos(phase_angle), jnp.sin(phase_angle))


def rotate(field_in, cosine, sine):
    rot_dims = cosine.shape[-1]
    half_rot = rot_dims // 2
    rot_part = field_in[..., :rot_dims]
    turned = jnp.concatenate([-rot_part[..., half_rot:], rot_part[..., :half_rot]], axis=-1)
    return jnp.concatenate([rot_part * cosine + turned * sine, field_in[..., rot_dims:]], axis=-1)


def unrotate(grad_field, cosine, sine):
    rot_dims = cosine.shape[-1]
    half_rot = rot_dims // 2
    sined = grad_field[..., :rot_dims] * sine
    turned_back = jnp.concatenate([sined[..., half_rot:], -sined[..., :half_rot]], axis=-1)
    return jnp.concatenate(
        [grad_field[..., :rot_dims] * cosine + turned_back, grad_field[..., rot_dims:]], axis=-1
    )


def doc_mask(segments):
    seq_len = segments.shape[1]
    token_index = jnp.arange(seq_len, dtype=jnp.int32)
    same_doc = segments[:, :, None] == segments[:, None, :]
    return jnp.logical_and(same_doc, (token_index[:, None] >= token_index[None, :])[None])


def attention_scores(queries, keys_rot, allowed):
    raw_scores = jnp.einsum(
        "rihd,rjhd->rhij", queries, keys_rot, preferred_element_type=jnp.float32
    )
    raw_scores = raw_scores * (1.0 / math.sqrt(HD))
    return jnp.where(allowed[:, None], raw_scores, -jnp.inf)


def forward(
    hidden_in,
    segments,
    positions,
    attn_gain,
    attn_shift,
    mlp_gain,
    mlp_shift,
    w_qkv,
    q_bias,
    v_bias,
    w_out,
    w_up,
    up_bias,
    w_down,
    out_bias,
):
    num_rows, seq_len = segments.shape
    model_width = hidden_in.shape[1]
    head_shape = (num_rows, seq_len, model_width // HD, HD)
    x_f32 = hidden_in.astype(jnp.float32)
    normed, inv_dev = normalize(x_f32)
    att_in = (normed * attn_gain.astype(jnp.float32) + attn_shift.astype(jnp.float32)).astype(
        jnp.bfloat16
    )
    mlp_in = (normed * mlp_gain.astype(jnp.float32) + mlp_shift.astype(jnp.float32)).astype(
        jnp.bfloat16
    )
    proj = jnp.dot(att_in, w_qkv, preferred_element_type=jnp.float32)
    cosine, sine = angles(positions, ROT)
    queries = rotate(
        (proj[:, :model_width] + q_bias.astype(jnp.float32)).reshape(head_shape), cosine, sine
    ).astype(jnp.bfloat16)
    keys_rot = rotate(
        proj[:, model_width : 2 * model_width].reshape(head_shape), cosine, sine
    ).astype(jnp.bfloat16)
    values = (
        (proj[:, 2 * model_width :] + v_bias.astype(jnp.float32))
        .astype(jnp.bfloat16)
        .reshape(head_shape)
    )
    allowed = doc_mask(segments)
    scores = attention_scores(queries, keys_rot, allowed)
    row_top = jnp.max(scores, axis=-1, keepdims=True)
    log_total = row_top + jnp.log(jnp.sum(jnp.exp(scores - row_top), axis=-1, keepdims=True))
    attn_probs = jnp.exp(scores - log_total).astype(jnp.bfloat16)
    head_mix = jnp.einsum("rhij,rjhd->rihd", attn_probs, values, preferred_element_type=jnp.float32)
    head_mix = head_mix.astype(jnp.bfloat16).reshape(num_rows * seq_len, model_width)
    attn_branch = jnp.dot(head_mix, w_out, preferred_element_type=jnp.float32)
    up_proj = jnp.dot(mlp_in, w_up, preferred_element_type=jnp.float32) + up_bias.astype(
        jnp.float32
    )
    activated = jax.nn.gelu(up_proj, approximate=False).astype(jnp.bfloat16)
    mlp_branch = jnp.dot(activated, w_down, preferred_element_type=jnp.float32)
    layer_out = (x_f32 + attn_branch + mlp_branch + out_bias.astype(jnp.float32)).astype(
        jnp.bfloat16
    )
    kept_state = (
        normed,
        inv_dev,
        att_in,
        mlp_in,
        queries,
        keys_rot,
        values,
        log_total,
        head_mix,
        up_proj,
        activated,
        cosine,
        sine,
        allowed,
    )
    return (layer_out, kept_state)


def backward(kept_state, cotangent, attn_gain, mlp_gain, w_qkv, w_out, w_up, w_down, grad_scale):
    (
        normed,
        inv_dev,
        att_in,
        mlp_in,
        queries,
        keys_rot,
        values,
        log_total,
        head_mix,
        up_proj,
        activated,
        cosine,
        sine,
        allowed,
    ) = kept_state
    head_shape = queries.shape
    total_rows, model_width = normed.shape
    cot_f32 = cotangent.astype(jnp.float32)
    grad_out_bias = grad_scale * jnp.sum(cot_f32, axis=0)
    grad_w_down = grad_scale * jnp.dot(activated.T, cotangent, preferred_element_type=jnp.float32)
    d_activated = jnp.dot(cotangent, w_down.T, preferred_element_type=jnp.float32)
    normal_cdf = 0.5 * (1.0 + lax.erf(up_proj * (1.0 / math.sqrt(2.0))))
    normal_pdf = jnp.exp(-0.5 * up_proj * up_proj) * (1.0 / math.sqrt(2.0 * math.pi))
    d_upper = d_activated * (normal_cdf + up_proj * normal_pdf)
    grad_up_bias = grad_scale * jnp.sum(d_upper, axis=0)
    d_upper16 = d_upper.astype(jnp.bfloat16)
    grad_w_up = grad_scale * jnp.dot(mlp_in.T, d_upper16, preferred_element_type=jnp.float32)
    d_mlp_in = jnp.dot(d_upper16, w_up.T, preferred_element_type=jnp.float32)
    grad_w_out = grad_scale * jnp.dot(head_mix.T, cotangent, preferred_element_type=jnp.float32)
    d_mix = (
        jnp.dot(cotangent, w_out.T, preferred_element_type=jnp.float32)
        .astype(jnp.bfloat16)
        .reshape(head_shape)
    )
    mix_heads = head_mix.reshape(head_shape)
    scores = attention_scores(queries, keys_rot, allowed)
    p_exact = jnp.exp(scores - log_total)
    attn_probs = p_exact.astype(jnp.bfloat16)
    d_values = jnp.einsum("rhij,rihd->rjhd", attn_probs, d_mix, preferred_element_type=jnp.float32)
    d_probs = jnp.einsum("rihd,rjhd->rhij", d_mix, values, preferred_element_type=jnp.float32)
    row_delta = jnp.sum(d_mix.astype(jnp.float32) * mix_heads.astype(jnp.float32), axis=-1)
    row_delta = jnp.transpose(row_delta, (0, 2, 1))[..., None]
    d_scores = (p_exact * (d_probs - row_delta) * (1.0 / math.sqrt(HD))).astype(jnp.bfloat16)
    d_queries = jnp.einsum(
        "rhij,rjhd->rihd", d_scores, keys_rot, preferred_element_type=jnp.float32
    )
    d_keys = jnp.einsum("rhij,rihd->rjhd", d_scores, queries, preferred_element_type=jnp.float32)
    d_q = unrotate(d_queries, cosine, sine).reshape(total_rows, model_width)
    d_k = unrotate(d_keys, cosine, sine).reshape(total_rows, model_width)
    d_v = d_values.reshape(total_rows, model_width)
    grad_q_bias = grad_scale * jnp.sum(d_q, axis=0)
    grad_v_bias = grad_scale * jnp.sum(d_v, axis=0)
    d_proj = jnp.concatenate([d_q, d_k, d_v], axis=1).astype(jnp.bfloat16)
    grad_w_qkv = grad_scale * jnp.dot(att_in.T, d_proj, preferred_element_type=jnp.float32)
    d_att_in = jnp.dot(d_proj, w_qkv.T, preferred_element_type=jnp.float32)
    grad_attn_gain = grad_scale * jnp.sum(d_att_in * normed, axis=0)
    grad_attn_shift = grad_scale * jnp.sum(d_att_in, axis=0)
    grad_mlp_gain = grad_scale * jnp.sum(d_mlp_in * normed, axis=0)
    grad_mlp_shift = grad_scale * jnp.sum(d_mlp_in, axis=0)
    d_normed = d_att_in * attn_gain.astype(jnp.float32) + d_mlp_in * mlp_gain.astype(jnp.float32)
    d_center = (
        d_normed
        - jnp.mean(d_normed, axis=-1, keepdims=True)
        - normed * jnp.mean(d_normed * normed, axis=-1, keepdims=True)
    )
    grad_in = (cot_f32 + inv_dev * d_center).astype(jnp.bfloat16)
    grads = (
        grad_attn_gain,
        grad_attn_shift,
        grad_mlp_gain,
        grad_mlp_shift,
        grad_w_qkv,
        grad_q_bias,
        grad_v_bias,
        grad_w_out,
        grad_w_up,
        grad_up_bias,
        grad_w_down,
        grad_out_bias,
    )
    return (grad_in, grads)


def local(
    hidden_in,
    segments,
    positions,
    attn_gain,
    attn_shift,
    mlp_gain,
    mlp_shift,
    w_qkv,
    q_bias,
    v_bias,
    w_out,
    w_up,
    up_bias,
    w_down,
    out_bias,
    cotangent,
):
    gathered = (
        lax.all_gather(attn_gain, "fsdp", axis=0, tiled=True),
        lax.all_gather(attn_shift, "fsdp", axis=0, tiled=True),
        lax.all_gather(mlp_gain, "fsdp", axis=0, tiled=True),
        lax.all_gather(mlp_shift, "fsdp", axis=0, tiled=True),
        lax.all_gather(w_qkv, "fsdp", axis=0, tiled=True),
        lax.all_gather(q_bias, "fsdp", axis=0, tiled=True),
        lax.all_gather(v_bias, "fsdp", axis=0, tiled=True),
        lax.all_gather(w_out, "fsdp", axis=0, tiled=True),
        lax.all_gather(w_up, "fsdp", axis=0, tiled=True),
        lax.all_gather(up_bias, "fsdp", axis=0, tiled=True),
        lax.all_gather(w_down, "fsdp", axis=0, tiled=True),
        lax.all_gather(out_bias, "fsdp", axis=0, tiled=True),
    )
    layer_out, kept_state = forward(
        hidden_in,
        segments,
        positions,
        gathered[0],
        gathered[1],
        gathered[2],
        gathered[3],
        gathered[4],
        gathered[5],
        gathered[6],
        gathered[7],
        gathered[8],
        gathered[9],
        gathered[10],
        gathered[11],
    )
    back_weights = (
        lax.all_gather(attn_gain, "fsdp", axis=0, tiled=True),
        lax.all_gather(mlp_gain, "fsdp", axis=0, tiled=True),
        lax.all_gather(w_qkv, "fsdp", axis=0, tiled=True),
        lax.all_gather(w_out, "fsdp", axis=0, tiled=True),
        lax.all_gather(w_up, "fsdp", axis=0, tiled=True),
        lax.all_gather(w_down, "fsdp", axis=0, tiled=True),
    )
    groups = lax.axis_size("fsdp")
    replicas = lax.axis_size("replica")
    grad_scale = 1.0 / math.sqrt(hidden_in.shape[0] * groups * replicas)
    grad_in, grads = backward(
        kept_state,
        cotangent,
        back_weights[0],
        back_weights[1],
        back_weights[2],
        back_weights[3],
        back_weights[4],
        back_weights[5],
        grad_scale,
    )
    shares = (
        lax.psum_scatter(
            grads[0].astype(jnp.bfloat16), "fsdp", scatter_dimension=0, tiled=True
        ).astype(jnp.float32),
        lax.psum_scatter(
            grads[1].astype(jnp.bfloat16), "fsdp", scatter_dimension=0, tiled=True
        ).astype(jnp.float32),
        lax.psum_scatter(
            grads[2].astype(jnp.bfloat16), "fsdp", scatter_dimension=0, tiled=True
        ).astype(jnp.float32),
        lax.psum_scatter(
            grads[3].astype(jnp.bfloat16), "fsdp", scatter_dimension=0, tiled=True
        ).astype(jnp.float32),
        lax.psum_scatter(
            grads[4].astype(jnp.bfloat16), "fsdp", scatter_dimension=0, tiled=True
        ).astype(jnp.float32),
        lax.psum_scatter(
            grads[5].astype(jnp.bfloat16), "fsdp", scatter_dimension=0, tiled=True
        ).astype(jnp.float32),
        lax.psum_scatter(
            grads[6].astype(jnp.bfloat16), "fsdp", scatter_dimension=0, tiled=True
        ).astype(jnp.float32),
        lax.psum_scatter(
            grads[7].astype(jnp.bfloat16), "fsdp", scatter_dimension=0, tiled=True
        ).astype(jnp.float32),
        lax.psum_scatter(
            grads[8].astype(jnp.bfloat16), "fsdp", scatter_dimension=0, tiled=True
        ).astype(jnp.float32),
        lax.psum_scatter(
            grads[9].astype(jnp.bfloat16), "fsdp", scatter_dimension=0, tiled=True
        ).astype(jnp.float32),
        lax.psum_scatter(
            grads[10].astype(jnp.bfloat16), "fsdp", scatter_dimension=0, tiled=True
        ).astype(jnp.float32),
        lax.psum_scatter(
            grads[11].astype(jnp.bfloat16), "fsdp", scatter_dimension=0, tiled=True
        ).astype(jnp.float32),
    )
    totals = (
        lax.psum(shares[0].astype(jnp.bfloat16), "replica").astype(jnp.float32),
        lax.psum(shares[1].astype(jnp.bfloat16), "replica").astype(jnp.float32),
        lax.psum(shares[2].astype(jnp.bfloat16), "replica").astype(jnp.float32),
        lax.psum(shares[3].astype(jnp.bfloat16), "replica").astype(jnp.float32),
        lax.psum(shares[4].astype(jnp.bfloat16), "replica").astype(jnp.float32),
        lax.psum(shares[5].astype(jnp.bfloat16), "replica").astype(jnp.float32),
        lax.psum(shares[6].astype(jnp.bfloat16), "replica").astype(jnp.float32),
        lax.psum(shares[7].astype(jnp.bfloat16), "replica").astype(jnp.float32),
        lax.psum(shares[8].astype(jnp.bfloat16), "replica").astype(jnp.float32),
        lax.psum(shares[9].astype(jnp.bfloat16), "replica").astype(jnp.float32),
        lax.psum(shares[10].astype(jnp.bfloat16), "replica").astype(jnp.float32),
        lax.psum(shares[11].astype(jnp.bfloat16), "replica").astype(jnp.float32),
    )
    return (
        layer_out,
        grad_in,
        totals[0],
        totals[1],
        totals[2],
        totals[3],
        totals[4],
        totals[5],
        totals[6],
        totals[7],
        totals[8],
        totals[9],
        totals[10],
        totals[11],
    )


def solution(mesh):
    placed = (
        P(("replica", "fsdp"), None),
        P(("replica", "fsdp"), None),
        P(("replica", "fsdp"), None),
        P("fsdp"),
        P("fsdp"),
        P("fsdp"),
        P("fsdp"),
        P("fsdp", None),
        P("fsdp"),
        P("fsdp"),
        P("fsdp", None),
        P("fsdp", None),
        P("fsdp"),
        P("fsdp", None),
        P("fsdp"),
        P(("replica", "fsdp"), None),
    )
    return jax.shard_map(
        local,
        mesh=mesh,
        in_specs=placed,
        out_specs=(
            P(("replica", "fsdp"), None),
            P(("replica", "fsdp"), None),
            P("fsdp"),
            P("fsdp"),
            P("fsdp"),
            P("fsdp"),
            P("fsdp", None),
            P("fsdp"),
            P("fsdp"),
            P("fsdp", None),
            P("fsdp", None),
            P("fsdp"),
            P("fsdp", None),
            P("fsdp"),
        ),
        check_vma=False,
    )
```

profile of v0, /device:TPU:0, one launch (start us, length us, event | category | flops | bytes accessed | tf_op | source)
XLA Modules:
  0.0 659.2 jit_solution(15322752099682157164)
XLA Ops:
  12.8 21.2 %all-reduce.18 = (bf16[768]{0:T(1024)(128)(2,1)}, bf16[768]{0:T(1024)(128)(2,1)}, bf16[768]{0:T(1024)(128)(2,1)S(1)}, bf16[768]{0:T(1024)(128)(2,1)S(1)}, bf16[7...) all-reduce(bf16[768]{0:T(1024)(128)(2,1)S(1)} %dynamic-update-slice, ...), channel_id=1, replica_groups=mesh['replica'=8,'fsdp'=4] {'fsdp'}, use_global_device_ids=true, to_apply=%add.5 | all-reduce | flops 4608 | bytes 18432
  34.9 8.2 %all-gather.8.cloned.1.call-done = bf16[768,768]{1,0:T(8,128)(2,1)} async-done(((bf16[192,768]{1,0:T(8,128)(2,1)}), bf16[768,768]{1,0:T(8,128)(2,1)}) %all-gather.8.cloned.1.call-update) | async-done | bytes 1179664 | tf_op jit(solution)/shard_map/all_gather | solution.py:246
  43.1 1.8 convolution_convert_fusion.1
  47.2 66.5 %all-gather.6.cloned.1.call-done = bf16[768,2304]{1,0:T(8,128)(2,1)} async-done(((bf16[192,2304]{1,0:T(8,128)(2,1)}), bf16[768,2304]{1,0:T(8,128)(2,1)}) %all-gather.6.cloned.1.call-update) | async-done | bytes 3538960 | tf_op jit(solution)/shard_map/all_gather | solution.py:243
  113.8 3.3 fusion.74
  119.6 1.6 copy.60
  127.1 2.9 multiply_convert_fusion.3
  132.8 1.8 multiply_convert_fusion.4
  134.9 1.7 convolution_bitcast_fusion.2
  137.8 4.0 fusion.79
  142.7 4.1 multiply_convert_fusion.2
  147.5 13.8 %all-gather = bf16[4,1,768]{2,1,0:T(2,128)(2,1)S(1)} all-gather(bf16[1,1,768]{2,1,0:T(2,128)(2,1)S(1)} %reshape.425), channel_id=1, replica_groups=mesh['replica'=8,'fsdp'=4] {'fsdp'}, dimensions={0}, use_global_device_ids=true | all-gather | bytes 7680 | tf_op jit(solution)/shard_map/all_gather | solution.py:248
  161.3 42.2 %all-gather.10.cloned.1.call-done = bf16[768,3072]{1,0:T(8,128)(2,1)} async-done(((bf16[192,3072]{1,0:T(8,128)(2,1)}), bf16[768,3072]{1,0:T(8,128)(2,1)}) %all-gather.10.cloned.1.call-update) | async-done | bytes 4718608 | tf_op jit(solution)/shard_map/all_gather | solution.py:247
  203.5 11.9 %fusion.3 = (bf16[288,3072]{1,0:T(8,128)(2,1)S(1)}, f32[288,3072]{1,0:T(8,128)}) fusion(f32[3072]{0:T(1024)S(1)} %bitcast.87, bf16[768,3072]{1,0:T(8,128)(2,1)} %all-gather.10.cloned.1.call-done, bf16[288,768]{1,0:T(8,128)(2,1)S(1)} %copy-done, f32[768]{0:T(1024)S(1)} %convert_element_type.223, f32[768]{0:T(1024)S(1)} %convert_element_type.222, ...), kind=kOutput, calls=%fused_computation.14 | convolution fusion | flops 1418674176 | bytes 10490112 | tf_op jit(solution)/shard_map/dot_general | solution.py:108
  216.6 4.3 multiply_convert_fusion
  221.2 71.6 %all-gather.12.cloned.1.call-done = bf16[3072,768]{1,0:T(8,128)(2,1)} async-done(((bf16[768,768]{1,0:T(8,128)(2,1)}), bf16[3072,768]{1,0:T(8,128)(2,1)}) %all-gather.12.cloned.1.call-update) | async-done | bytes 4718608 | tf_op jit(solution)/shard_map/all_gather | solution.py:249
  292.8 6.4 fusion.83
  300.4 4.8 multiply_convert_fusion.1
  307.2 3.9 fusion.44
  311.1 4.4 fusion.78
  316.7 6.5 reduce-scatter.7.cloned.1.call-done
  323.3 67.3 %reduce-scatter.5.cloned.1.call-done = bf16[192,2304]{1,0:T(8,128)(2,1)} async-done(((bf16[768,2304]{1,0:T(8,128)(2,1)}), bf16[192,2304]{1,0:T(8,128)(2,1)}) %reduce-scatter.5.cloned.1.call-update) | async-done | bytes 884752 | tf_op jit(solution)/shard_map/reduce_scatter | solution.py:304
  390.6 87.8 %reduce-scatter.11.cloned.1.call-done = bf16[768,768]{1,0:T(8,128)(2,1)} async-done(((bf16[3072,768]{1,0:T(8,128)(2,1)}), bf16[768,768]{1,0:T(8,128)(2,1)}) %reduce-scatter.11.cloned.1.call-update) | async-done | bytes 1179664 | tf_op jit(solution)/shard_map/reduce_scatter | solution.py:322
  478.4 88.1 %reduce-scatter.9.cloned.1.call-done = bf16[192,3072]{1,0:T(8,128)(2,1)} async-done(((bf16[768,3072]{1,0:T(8,128)(2,1)}), bf16[192,3072]{1,0:T(8,128)(2,1)}) %reduce-scatter.9.cloned.1.call-update) | async-done | bytes 1179664 | tf_op jit(solution)/shard_map/reduce_scatter | solution.py:316
  566.6 18.2 %all-reduce.17 = (bf16[768]{0:T(1024)(128)(2,1)S(1)}, bf16[768]{0:T(1024)(128)(2,1)S(1)}, bf16[768]{0:T(1024)(128)(2,1)S(1)}, bf16[768]{0:T(1024)(128)(2,1)S(1)}...) all-reduce(bf16[768]{0:T(1024)(128)(2,1)S(1)} %dynamic-update-slice, ...), channel_id=1, replica_groups=mesh['replica'=8,'fsdp'=4] {'fsdp'}, use_global_device_ids=true, to_apply=%add.6 | all-reduce | flops 9216 | bytes 36864
  585.4 12.4 %all-reduce.15 = (bf16[192]{0:T(256)(128)(2,1)S(1)}, bf16[192]{0:T(256)(128)(2,1)S(1)}, bf16[192]{0:T(256)(128)(2,1)S(1)}, bf16[192]{0:T(256)(128)(2,1)S(1)}, bf...) all-reduce(bf16[192]{0:T(256)(128)(2,1)S(1)} %dynamic-slice.8, ...), channel_id=1, replica_groups=mesh['replica'=8,'fsdp'=4] {'replica'}, use_global_device_ids=true, to_apply=%region_9.10 | all-reduce | flops 2112 | bytes 8448 | tf_op jit(solution)/shard_map/psum | solution.py:330
  602.4 4.0 fusion.84
  607.8 37.1 %all-reduce.21.cloned.1.call-done = (bf16[192,2304]{1,0:T(8,128)(2,1)}, bf16[192,768]{1,0:T(8,128)(2,1)}, bf16[192,3072]{1,0:T(8,128)(2,1)}, bf16[768,768]{1,0:T(8,128)(2,1)}) async-done(((bf16[192,2304]{1,0:T(8,128)(2,1)}, bf16[192,768]{1,0:T(8,128)(2,1)}, bf16[192,3072]{1,0:T(8,128)(2,1)}, bf16[768,768]{1,0:T(8,128)(2,1)}), (bf16[192,2304]{1,0:T(8,128)(2,1)}, bf16[192,768]{1,0:T(8,128)(2,1)}, ...) | async-done | bytes 3538960 | tf_op jit(solution)/shard_map/psum | solution.py:334
  645.0 2.0 convert_element_type.254
  646.9 2.5 convert_element_type.246
  649.4 1.7 convert_element_type.256
  651.1 1.6 convert_element_type.260
  (192 shorter events, 33.0 us)
Async XLA Ops:
  7.2 4.2 copy-start.32
  7.2 4.5 copy-start.33
  7.2 4.7 copy-start.34
  7.2 4.9 copy-start.35
  7.2 5.1 copy-start.36
  7.2 5.4 copy-start.37
  7.3 26.8 %copy-start.31 = (s32[1,288]{1,0:T(1,128)S(1)}, s32[1,288]{1,0:T(1,128)}, u32[]{:S(2)}) copy-start(s32[1,288]{1,0:T(1,128)} %param.17) | copy-start | bytes 3460
  7.3 26.8 %copy-start.30 = (s32[1,288]{1,0:T(1,128)S(1)}, s32[1,288]{1,0:T(1,128)}, u32[]{:S(2)}) copy-start(s32[1,288]{1,0:T(1,128)} %param.18) | copy-start | bytes 3460
  7.3 27.0 %copy-start = (bf16[288,768]{1,0:T(8,128)(2,1)S(1)}, bf16[288,768]{1,0:T(8,128)(2,1)}, u32[]{:S(2)}) copy-start(bf16[288,768]{1,0:T(8,128)(2,1)} %param.16) | copy-start | bytes 1327108
  7.3 35.8 %copy-start.17 = (bf16[288,768]{1,0:T(8,128)(2,1)S(1)}, bf16[288,768]{1,0:T(8,128)(2,1)}, u32[]{:S(2)}) copy-start(bf16[288,768]{1,0:T(8,128)(2,1)} %param.31) | copy-start | bytes 1327108
  7.3 35.8 %all-gather.8.cloned.1.call-start = ((), (), s32[]{:S(2)}) async-start(), calls=%async_computation.5 | async-start | bytes 1474560 | tf_op jit(solution)/shard_map/all_gather | solution.py:246
  8.0 105.7 %all-gather.6.cloned.1.call-start = ((), (), s32[]{:S(2)}) async-start(), calls=%async_computation.4 | async-start | bytes 4423680 | tf_op jit(solution)/shard_map/all_gather | solution.py:243
  8.8 194.7 %all-gather.10.cloned.1.call-start = ((), (), s32[]{:S(2)}) async-start(), calls=%async_computation.6 | async-start | bytes 5898240 | tf_op jit(solution)/shard_map/all_gather | solution.py:247
  9.5 283.2 %all-gather.12.cloned.1.call-start = ((), (), s32[]{:S(2)}) async-start(), calls=%async_computation.7 | async-start | bytes 5898240 | tf_op jit(solution)/shard_map/all_gather | solution.py:249
  10.1 313.2 %reduce-scatter.7.cloned.1.call-start = ((), (), s32[]{:S(2)}) async-start(), calls=%async_computation.9 | async-start | bytes 1474560 | tf_op jit(solution)/shard_map/reduce_scatter | solution.py:313
  34.3 87.0 %copy-start.20 = (f32[288,16]{0,1:T(8,128)}, f32[288,16]{0,1:T(8,128)S(1)}, u32[]{:S(2)}) copy-start(f32[288,16]{0,1:T(8,128)S(1)} %get-tuple-element.73) | copy-start | bytes 55300
  34.3 87.0 %copy-start.22 = (f32[288,16]{0,1:T(8,128)}, f32[288,16]{0,1:T(8,128)S(1)}, u32[]{:S(2)}) copy-start(f32[288,16]{0,1:T(8,128)S(1)} %get-tuple-element.74) | copy-start | bytes 55300
  34.9 89.0 %copy-start.15 = (pred[288,288]{0,1:T(8,128)(4,1)}, pred[288,288]{0,1:T(8,128)(4,1)S(1)}, u32[]{:S(2)}) copy-start(pred[288,288]{0,1:T(8,128)(4,1)S(1)} %fusion.47) | copy-start | bytes 248836
  122.6 4.4 copy-start.1
  123.8 3.2 copy-start.24
  127.0 5.8 copy-start.13
  134.7 255.9 %reduce-scatter.5.cloned.1.call-start = ((), (), s32[]{:S(2)}) async-start(), calls=%async_computation.8 | async-start | bytes 4423680 | tf_op jit(solution)/shard_map/reduce_scatter | solution.py:304
  146.8 331.6 %reduce-scatter.11.cloned.1.call-start = ((), (), s32[]{:S(2)}) async-start(), calls=%async_computation.11 | async-start | bytes 5898240 | tf_op jit(solution)/shard_map/reduce_scatter | solution.py:322
  203.5 13.1 %copy-start.19 = (bf16[288,768]{1,0:T(8,128)(2,1)S(1)}, bf16[288,768]{1,0:T(8,128)(2,1)}, u32[]{:S(2)}) copy-start(bf16[288,768]{1,0:T(8,128)(2,1)} %param.31) | copy-start | bytes 1327108
  220.9 345.6 %reduce-scatter.9.cloned.1.call-start = ((), (), s32[]{:S(2)}) async-start(), calls=%async_computation.10 | async-start | bytes 5898240 | tf_op jit(solution)/shard_map/reduce_scatter | solution.py:316
  305.2 339.8 %all-reduce.21.cloned.1.call-start = ((), (), s32[]{:S(2)}) async-start(), calls=%async_computation.12 | async-start | bytes 7077888 | tf_op jit(solution)/shard_map/psum | solution.py:334
  307.2 3.9 copy-start.41
  315.5 286.9 %copy-start.43 = (bf16[288,3072]{1,0:T(8,128)(2,1)S(1)}, bf16[288,3072]{1,0:T(8,128)(2,1)}, u32[]{:S(2)}) copy-start(bf16[288,3072]{1,0:T(8,128)(2,1)} %copy-done.42) | copy-start | bytes 5308420
  602.4 4.1 copy-start.8
  602.4 4.1 copy-start.14
  645.0 4.5 copy-start.6
  645.0 6.1 copy-start.5
  (21 other events, 31.3 us)
Sparse Core Ops, SparseCore 0:
  9.7 33.3 all-gather.7
  44.7 69.0 all-gather.5
  115.3 88.1 all-gather.9
  204.9 87.7 all-gather.11
  295.5 27.7 reduce-scatter.6
  325.4 65.0 reduce-scatter.4
  392.9 85.4 reduce-scatter.10
  480.7 85.7 reduce-scatter.8
  570.2 74.7 all-reduce.20
where the time goes:
time: 660 us; the launch traced here: 659 us
  waiting for transfers between devices  478 us (72%)
  blocking collectives  65.6 us (10%)
  matrix products  64.4 us (10%)
  other arithmetic  17.2 us (3%)
  local copies, waits for them, and re-layouts  16.7 us (3%)
  between operations  16.5 us (2%)
    reduce_scatter x1, waiting for transfers between devices, local(): lax.psum_scatter(grads[8].astype(jnp.bfloat16), 'fsdp', scatter_dimension...  88.1 us
    reduce_scatter x1, waiting for transfers between devices, local(): lax.psum_scatter(grads[10].astype(jnp.bfloat16), 'fsdp', scatter_dimensio...  87.8 us
    all_gather x1, waiting for transfers between devices, local(): lax.all_gather(w_down, 'fsdp', axis=0, tiled=True)  71.6 us
    reduce_scatter x1, waiting for transfers between devices, local(): lax.psum_scatter(grads[4].astype(jnp.bfloat16), 'fsdp', scatter_dimension...  67.3 us
    all_gather x1, waiting for transfers between devices, local(): lax.all_gather(w_qkv, 'fsdp', axis=0, tiled=True)  66.5 us
    all_gather x1, waiting for transfers between devices, local(): lax.all_gather(w_up, 'fsdp', axis=0, tiled=True)  42.2 us
    unnamed x2, blocking collectives  39.4 us
    psum x1, waiting for transfers between devices, local(): lax.psum(shares[4].astype(jnp.bfloat16), 'replica').astype(jnp.float32)  37.1 us
  transfers between devices with their start and end apart: 9, of which 9 were waited for; matrix products, arithmetic and copies ran while one was open for 13% of the time, Pallas kernels for 0%

commit v1 on v0

--- a/solution.py
+++ b/solution.py
@@ -331,7 +331,9 @@
         lax.psum(shares[1].astype(jnp.bfloat16), "replica").astype(jnp.float32),
         lax.psum(shares[2].astype(jnp.bfloat16), "replica").astype(jnp.float32),
         lax.psum(shares[3].astype(jnp.bfloat16), "replica").astype(jnp.float32),
-        lax.psum(shares[4].astype(jnp.bfloat16), "replica").astype(jnp.float32),
+        jnp.sum(lax.all_gather(shares[4].astype(jnp.bfloat16), "replica"), axis=0).astype(
+            jnp.float32
+        ),
         lax.psum(shares[5].astype(jnp.bfloat16), "replica").astype(jnp.float32),
         lax.psum(shares[6].astype(jnp.bfloat16), "replica").astype(jnp.float32),
         lax.psum(shares[7].astype(jnp.bfloat16), "replica").astype(jnp.float32),

time: 660 us -> 700 us (1.061)
  waiting for transfers between devices: 478 us -> 513 us
  other arithmetic: 17.2 us -> 24.8 us
    all_gather x0 -> x1, waiting for transfers between devices: none -> 43.6 us  [local(): lax.all_gather(shares[4].astype(jnp.bfloat16), 'replica')]
    all_gather x1, waiting for transfers between devices: 42.2 us -> 72.4 us  [local(): lax.all_gather(w_up, 'fsdp', axis=0, tiled=True)]
    psum x1, waiting for transfers between devices: 37.1 us -> 17.6 us  [local(): lax.psum(shares[7].astype(jnp.bfloat16), 'replica').astype(jnp.float32)]
    all_gather x1, waiting for transfers between devices: 8.21 us -> 0.01 us  [local(): lax.all_gather(w_out, 'fsdp', axis=0, tiled=True)]
  transfers between devices with their start and end apart: 9 -> 10, of which waited for: 9 -> 9; matrix products, arithmetic and copies ran while one was open for 13% -> 13% of each run, Pallas kernels for 0% -> 0%
where the time goes in v1:
time: 700 us; the launch traced here: 699 us
  waiting for transfers between devices  513 us (73%)
  blocking collectives  64.5 us (9%)
  matrix products  63.6 us (9%)
  other arithmetic  24.8 us (4%)
  between operations  16.9 us (2%)
  local copies, waits for them, and re-layouts  15.4 us (2%)
    reduce_scatter x1, waiting for transfers between devices, local(): lax.psum_scatter(grads[8].astype(jnp.bfloat16), 'fsdp', scatter_dimension...  88.1 us
    reduce_scatter x1, waiting for transfers between devices, local(): lax.psum_scatter(grads[10].astype(jnp.bfloat16), 'fsdp', scatter_dimensio...  86.1 us
    all_gather x1, waiting for transfers between devices, local(): lax.all_gather(w_up, 'fsdp', axis=0, tiled=True)  72.4 us
    all_gather x1, waiting for transfers between devices, local(): lax.all_gather(w_down, 'fsdp', axis=0, tiled=True)  71.8 us
    reduce_scatter x1, waiting for transfers between devices, local(): lax.psum_scatter(grads[4].astype(jnp.bfloat16), 'fsdp', scatter_dimension...  69.3 us
    all_gather x1, waiting for transfers between devices, local(): lax.all_gather(w_qkv, 'fsdp', axis=0, tiled=True)  60.1 us
    all_gather x1, waiting for transfers between devices, local(): lax.all_gather(shares[4].astype(jnp.bfloat16), 'replica')  43.6 us
    unnamed x2, blocking collectives  39.1 us
  transfers between devices with their start and end apart: 10, of which 9 were waited for; matrix products, arithmetic and copies ran while one was open for 13% of the time, Pallas kernels for 0%

profile of v1, /device:TPU:0, one launch (start us, length us, event | category | flops | bytes accessed | tf_op | source)
XLA Modules:
  0.0 699.3 jit_solution(4938898871555455723)
XLA Ops:
  12.8 21.2 %all-reduce.18 = (bf16[768]{0:T(1024)(128)(2,1)S(1)}, bf16[768]{0:T(1024)(128)(2,1)S(1)}, bf16[768]{0:T(1024)(128)(2,1)S(1)}, bf16[768]{0:T(1024)(128)(2,1)S(1)}...) all-reduce(bf16[768]{0:T(1024)(128)(2,1)S(1)} %dynamic-update-slice, ...), channel_id=1, replica_groups=mesh['replica'=8,'fsdp'=4] {'fsdp'}, use_global_device_ids=true, to_apply=%add.5 | all-reduce | flops 4608 | bytes 18432
  35.3 13.3 %all-gather.1 = bf16[4,1,768]{2,1,0:T(2,128)(2,1)S(1)} all-gather(bf16[1,1,768]{2,1,0:T(2,128)(2,1)S(1)} %reshape.426), channel_id=1, replica_groups=mesh['replica'=8,'fsdp'=4] {'fsdp'}, dimensions={0}, use_global_device_ids=true | all-gather | bytes 7680 | tf_op jit(solution)/shard_map/all_gather | solution.py:248
  50.6 1.9 convolution_convert_fusion.1
  53.8 60.1 %all-gather.8.cloned.1.call-done = bf16[768,2304]{1,0:T(8,128)(2,1)} async-done(((bf16[192,2304]{1,0:T(8,128)(2,1)}), bf16[768,2304]{1,0:T(8,128)(2,1)}) %all-gather.8.cloned.1.call-update) | async-done | bytes 3538960 | tf_op jit(solution)/shard_map/all_gather | solution.py:243
  113.9 3.3 fusion.74
  119.8 1.6 copy.60
  122.5 2.2 fusion.15
  129.1 1.8 multiply_convert_fusion.4
  131.1 72.4 %all-gather.12.cloned.1.call-done = bf16[768,3072]{1,0:T(8,128)(2,1)} async-done(((bf16[192,3072]{1,0:T(8,128)(2,1)}), bf16[768,3072]{1,0:T(8,128)(2,1)}) %all-gather.12.cloned.1.call-update) | async-done | bytes 4718608 | tf_op jit(solution)/shard_map/all_gather | solution.py:247
  203.5 11.9 %fusion.3 = (bf16[288,3072]{1,0:T(8,128)(2,1)S(1)}, f32[288,3072]{1,0:T(8,128)}) fusion(f32[3072]{0:T(1024)S(1)} %bitcast.91, bf16[768,3072]{1,0:T(8,128)(2,1)} %all-gather.12.cloned.1.call-done, bf16[288,768]{1,0:T(8,128)(2,1)S(1)} %copy-done, f32[768]{0:T(1024)S(1)} %copy-done.27, f32[768]{0:T(1024)S(1)} %copy-done.22, f32[288]{0:T(512)S(1)} %copy-done.21, ...), kind=kOutput, calls=%fused_computation.14 | convolution fusion | flops 1418674176 | bytes 10490112 | tf_op jit(solution)/shard_map/dot_general | solution.py:108
  216.6 4.3 multiply_convert_fusion
  221.0 71.8 %all-gather.14.cloned.1.call-done = bf16[3072,768]{1,0:T(8,128)(2,1)} async-done(((bf16[768,768]{1,0:T(8,128)(2,1)}), bf16[3072,768]{1,0:T(8,128)(2,1)}) %all-gather.14.cloned.1.call-update) | async-done | bytes 4718608 | tf_op jit(solution)/shard_map/all_gather | solution.py:249
  292.8 6.4 fusion.83
  300.4 4.6 multiply_convert_fusion.1
  306.4 4.6 multiply_convert_fusion.3
  313.4 1.8 slice-done.1
  317.6 4.0 multiply_convert_fusion.2
  321.7 1.5 reduce-scatter.7.cloned.1.call-done
  323.3 86.1 %reduce-scatter.11.cloned.1.call-done = bf16[768,768]{1,0:T(8,128)(2,1)} async-done(((bf16[3072,768]{1,0:T(8,128)(2,1)}), bf16[768,768]{1,0:T(8,128)(2,1)}) %reduce-scatter.11.cloned.1.call-update) | async-done | bytes 1179664 | tf_op jit(solution)/shard_map/reduce_scatter | solution.py:322
  409.3 88.1 %reduce-scatter.9.cloned.1.call-done = bf16[192,3072]{1,0:T(8,128)(2,1)} async-done(((bf16[768,3072]{1,0:T(8,128)(2,1)}), bf16[192,3072]{1,0:T(8,128)(2,1)}) %reduce-scatter.9.cloned.1.call-update) | async-done | bytes 1179664 | tf_op jit(solution)/shard_map/reduce_scatter | solution.py:316
  497.6 69.3 %reduce-scatter.5.cloned.1.call-done = bf16[192,2304]{1,0:T(8,128)(2,1)} async-done(((bf16[768,2304]{1,0:T(8,128)(2,1)}), bf16[192,2304]{1,0:T(8,128)(2,1)}) %reduce-scatter.5.cloned.1.call-update) | async-done | bytes 884752 | tf_op jit(solution)/shard_map/reduce_scatter | solution.py:304
  568.8 3.9 fusion.44
  572.8 4.5 fusion.78
  578.5 17.9 %all-reduce.17 = (bf16[768]{0:T(1024)(128)(2,1)S(1)}, bf16[768]{0:T(1024)(128)(2,1)S(1)}, bf16[768]{0:T(1024)(128)(2,1)S(1)}, bf16[768]{0:T(1024)(128)(2,1)S(1)}...) all-reduce(bf16[768]{0:T(1024)(128)(2,1)S(1)} %dynamic-update-slice, ...), channel_id=1, replica_groups=mesh['replica'=8,'fsdp'=4] {'fsdp'}, use_global_device_ids=true, to_apply=%add.6 | all-reduce | flops 9216 | bytes 36864
  597.1 12.1 %all-reduce.15 = (bf16[192]{0:T(256)(128)(2,1)S(1)}, bf16[192]{0:T(256)(128)(2,1)S(1)}, bf16[192]{0:T(256)(128)(2,1)S(1)}, bf16[192]{0:T(256)(128)(2,1)S(1)}, bf...) all-reduce(bf16[192]{0:T(256)(128)(2,1)S(1)} %dynamic-slice.8, ...), channel_id=1, replica_groups=mesh['replica'=8,'fsdp'=4] {'replica'}, use_global_device_ids=true, to_apply=%region_9.10 | all-reduce | flops 2112 | bytes 8448 | tf_op jit(solution)/shard_map/psum | solution.py:330
  613.7 4.0 fusion.84
  619.1 17.6 %all-reduce.21.cloned.1.call-done = (bf16[192,768]{1,0:T(8,128)(2,1)}, bf16[192,3072]{1,0:T(8,128)(2,1)}, bf16[768,768]{1,0:T(8,128)(2,1)}) async-done(((bf16[192,768]{1,0:T(8,128)(2,1)}, bf16[192,3072]{1,0:T(8,128)(2,1)}, bf16[768,768]{1,0:T(8,128)(2,1)}), (bf16[192,768]{1,0:T(8,128)(2,1)}, bf16[192,3072]{1,0:T(8,128)(2,1)}, bf16[768,768]{1,0:T(8,128)(2,1)})) %all-reduce.21.cloned.1.call-update) | async-done | bytes 2654224 | tf_op jit(solution)/shard_map/psum | solution.py:339
  636.7 1.9 convert_element_type.256
  638.6 2.9 convert_element_type.258
  641.5 1.6 convert_element_type.262
  643.1 43.6 %all-gather.16.cloned.1.call-done = bf16[1536,2304]{1,0:T(8,128)(2,1)} async-done(((bf16[192,2304]{1,0:T(8,128)(2,1)}), bf16[1536,2304]{1,0:T(8,128)(2,1)}) %all-gather.16.cloned.1.call-update) | async-done | bytes 7077904 | tf_op jit(solution)/shard_map/all_gather | solution.py:334
  686.7 4.4 reduce_sum.151
  (201 shorter events, 35.6 us)
Async XLA Ops:
  7.2 4.7 copy-start.34
  7.2 4.9 copy-start.35
  7.2 5.1 copy-start.36
  7.2 5.4 copy-start.37
  7.3 27.4 %copy-start.29 = (bf16[768]{0:T(1024)(128)(2,1)S(1)}, bf16[768]{0:T(1024)(128)(2,1)}, u32[]{:S(2)}) copy-start(bf16[768]{0:T(1024)(128)(2,1)} %param.28) | copy-start | bytes 4612
  7.3 41.3 %copy-start.31 = (s32[1,288]{1,0:T(1,128)S(1)}, s32[1,288]{1,0:T(1,128)}, u32[]{:S(2)}) copy-start(s32[1,288]{1,0:T(1,128)} %param.17) | copy-start | bytes 3460
  7.3 41.3 %copy-start.30 = (s32[1,288]{1,0:T(1,128)S(1)}, s32[1,288]{1,0:T(1,128)}, u32[]{:S(2)}) copy-start(s32[1,288]{1,0:T(1,128)} %param.18) | copy-start | bytes 3460
  7.3 42.1 %copy-start = (bf16[288,768]{1,0:T(8,128)(2,1)S(1)}, bf16[288,768]{1,0:T(8,128)(2,1)}, u32[]{:S(2)}) copy-start(bf16[288,768]{1,0:T(8,128)(2,1)} %param.16) | copy-start | bytes 1327108
  7.3 43.3 %copy-start.15 = (bf16[288,768]{1,0:T(8,128)(2,1)S(1)}, bf16[288,768]{1,0:T(8,128)(2,1)}, u32[]{:S(2)}) copy-start(bf16[288,768]{1,0:T(8,128)(2,1)} %param.31) | copy-start | bytes 1327108
  7.3 43.3 %all-gather.10.cloned.1.call-start = ((), (), s32[]{:S(2)}) async-start(), calls=%async_computation.5 | async-start | bytes 1474560 | tf_op jit(solution)/shard_map/all_gather | solution.py:246
  8.0 105.9 %all-gather.8.cloned.1.call-start = ((), (), s32[]{:S(2)}) async-start(), calls=%async_computation.4 | async-start | bytes 4423680 | tf_op jit(solution)/shard_map/all_gather | solution.py:243
  8.8 194.7 %all-gather.12.cloned.1.call-start = ((), (), s32[]{:S(2)}) async-start(), calls=%async_computation.6 | async-start | bytes 5898240 | tf_op jit(solution)/shard_map/all_gather | solution.py:247
  9.5 283.3 %all-gather.14.cloned.1.call-start = ((), (), s32[]{:S(2)}) async-start(), calls=%async_computation.7 | async-start | bytes 5898240 | tf_op jit(solution)/shard_map/all_gather | solution.py:249
  10.1 313.2 %reduce-scatter.7.cloned.1.call-start = ((), (), s32[]{:S(2)}) async-start(), calls=%async_computation.9 | async-start | bytes 1474560 | tf_op jit(solution)/shard_map/reduce_scatter | solution.py:313
  35.2 82.0 %copy-start.23 = (f32[768]{0:T(1024)}, f32[768]{0:T(1024)S(1)}, u32[]{:S(2)}) copy-start(f32[768]{0:T(1024)S(1)} %convert_element_type.212) | copy-start | bytes 9220
  35.2 82.0 %copy-start.25 = (f32[768]{0:T(1024)}, f32[768]{0:T(1024)S(1)}, u32[]{:S(2)}) copy-start(f32[768]{0:T(1024)S(1)} %convert_element_type.213) | copy-start | bytes 9220
  49.9 67.4 %copy-start.20 = (f32[288]{0:T(512)}, f32[288]{0:T(512)S(1)}, u32[]{:S(2)}) copy-start(f32[288]{0:T(512)S(1)} %add_rsqrt_fusion) | copy-start | bytes 3460
  52.6 64.7 %copy-start.4 = (bf16[288,768]{1,0:T(8,128)(2,1)}, bf16[288,768]{1,0:T(8,128)(2,1)S(1)}, u32[]{:S(2)}) copy-start(bf16[288,768]{1,0:T(8,128)(2,1)S(1)} %convolution_convert_fusion.1) | copy-start | bytes 1327108
  129.0 86.4 %copy-start.12 = (bf16[12,64,288]{2,1,0:T(8,128)(2,1)}, bf16[12,64,288]{2,1,0:T(8,128)(2,1)S(1)}, u32[]{:S(2)}) copy-start(bf16[12,64,288]{2,1,0:T(8,128)(2,1)S(1)} %get-tuple-element.82) | copy-start | bytes 1327108
  129.0 74.5 %copy-start.21 = (f32[288]{0:T(512)S(1)}, f32[288]{0:T(512)}, u32[]{:S(2)}) copy-start(f32[288]{0:T(512)} %copy-done.20) | copy-start | bytes 3460
  129.0 74.5 %copy-start.22 = (f32[768]{0:T(1024)S(1)}, f32[768]{0:T(1024)}, u32[]{:S(2)}) copy-start(f32[768]{0:T(1024)} %convert_element_type.224) | copy-start | bytes 9220
  129.0 74.5 %copy-start.27 = (f32[768]{0:T(1024)S(1)}, f32[768]{0:T(1024)}, u32[]{:S(2)}) copy-start(f32[768]{0:T(1024)} %convert_element_type.225) | copy-start | bytes 9220
  130.9 278.5 %reduce-scatter.11.cloned.1.call-start = ((), (), s32[]{:S(2)}) async-start(), calls=%async_computation.11 | async-start | bytes 5898240 | tf_op jit(solution)/shard_map/reduce_scatter | solution.py:322
  220.9 276.6 %reduce-scatter.9.cloned.1.call-start = ((), (), s32[]{:S(2)}) async-start(), calls=%async_computation.10 | async-start | bytes 5898240 | tf_op jit(solution)/shard_map/reduce_scatter | solution.py:316
  305.1 261.8 %reduce-scatter.5.cloned.1.call-start = ((), (), s32[]{:S(2)}) async-start(), calls=%async_computation.8 | async-start | bytes 4423680 | tf_op jit(solution)/shard_map/reduce_scatter | solution.py:304
  306.4 4.7 copy-start.10
  306.4 4.7 copy-start.3
  321.7 246.6 %copy-start.38 = (bf16[192]{0:T(256)(128)(2,1)S(1)}, bf16[192]{0:T(256)(128)(2,1)}, u32[]{:S(2)}) copy-start(bf16[192]{0:T(256)(128)(2,1)} %param.30) | copy-start | bytes 1156
  321.7 315.0 %all-reduce.21.cloned.1.call-start = ((), (), s32[]{:S(2)}) async-start(), calls=%async_computation.13 | async-start | bytes 5308416 | tf_op jit(solution)/shard_map/psum | solution.py:339
  497.5 189.2 %all-gather.16.cloned.1.call-start = ((), (), s32[]{:S(2)}) async-start(), calls=%async_computation.12 | async-start | bytes 7962624 | tf_op jit(solution)/shard_map/all_gather | solution.py:334
  572.8 41.0 %copy-start.43 = (bf16[288,3072]{1,0:T(8,128)(2,1)S(1)}, bf16[288,3072]{1,0:T(8,128)(2,1)}, u32[]{:S(2)}) copy-start(bf16[288,3072]{1,0:T(8,128)(2,1)} %copy-done.42) | copy-start | bytes 5308420
  636.7 4.9 copy-start.6
  (24 other events, 60.2 us)
Sparse Core Ops, SparseCore 0:
  9.7 33.5 all-gather.9
  44.8 69.0 all-gather.7
  115.5 87.9 all-gather.11
  204.9 87.7 all-gather.13
  295.5 27.7 reduce-scatter.6
  325.4 83.8 reduce-scatter.10
  411.6 85.7 reduce-scatter.8
  499.8 67.0 reduce-scatter.4
  570.5 66.1 all-reduce.20
  638.4 48.2 all-gather.15
